TPU v7x, 512 devices: a whole 4x8x8 slice. The times are simulated.
512 devices in a mesh: occ: 128 (over y, z, core), virt: 4 (over x).
Axes of the slice: x: 4, y: 8, z: 8, core: 2. Of those that a mesh axis runs over, the one named last changes fastest.
Arguments:
- factors: bfloat16 [768, 98304], P('virt', 'occ'), may hold values from -1 to 1
- occ_energy: float32 [64], replicated, may hold values from -2 to -0.5
- virt_energy: float32 [768], replicated, may hold values from 0.2 to 3
- pair_table: int32 [256, 2], P('occ'), may hold values from 0 to 63, as said below
- pair_count: int32 [128], P('occ'), may hold values from 0 to 2, as said below
Outputs:
- gamma: float32 [768, 98304], P('virt', 'occ')
Inputs may be any that keep to these rules, and one draw needn't show every extreme that they name: `pair_table`: each row holds two different orbitals. `pair_count`: the counts sum to exactly 128, and some host has exactly 2.
All inputs are finite; a program needn't handle non-finite values.
Results may differ from a plain program's by a relative error of at most 0.0029.
Values may be sent and summed in bfloat16 or wider, within the bound.
A program may use at most 64 MiB of HBM per device.

v0:
```python
import jax
import jax.numpy as jnp
from jax import lax
from jax.sharding import PartitionSpec as P


def laid_out(blocks, dim):
    dims = list(blocks.shape[1:])
    dims[dim] *= blocks.shape[0]
    return jnp.moveaxis(blocks, 0, dim).reshape(dims)


def gather_together(arrays, axis, dims):
    ravelled = jnp.concatenate([a.reshape(-1) for a in arrays])
    lines, at, finished = (lax.all_gather(ravelled, axis), 0, [])
    for a, dim in zip(arrays, dims):
        blocks = lines[:, at : at + a.size].reshape(-1, *a.shape)
        finished.append(laid_out(blocks, dim))
        at += a.size
    return tuple(finished)


def body(factors, occ_energy, virt_energy, pair_table, pair_count):
    tables, counts = gather_together((pair_table, pair_count), "occ", (0, 0))
    hosts_total = lax.axis_size("occ")
    per_host = pair_table.shape[0]
    entries = jnp.arange(hosts_total * per_host, dtype=jnp.int32)
    active = entries % per_host < jnp.repeat(counts, per_host)
    live_total = per_host * hosts_total // 2
    slot_count = -(-live_total // hosts_total)
    ranking = jnp.cumsum(active.astype(jnp.int32)) - 1
    targets = jnp.arange(hosts_total * slot_count, dtype=jnp.int32)
    select = (active[None, :] & (ranking[None, :] == targets[:, None])).astype(jnp.int32)
    plan = jnp.sum(select[:, :, None] * tables[None, :, :], axis=1).reshape(
        hosts_total, slot_count, 2
    )
    enabled = jnp.max(select, axis=1).reshape(hosts_total, slot_count)
    column = lax.axis_index("virt")
    myself = lax.axis_index("occ")
    orbital_count = occ_energy.shape[0]
    slab_width = factors.shape[0]
    aux_local = factors.shape[1] // orbital_count
    slab_energy = lax.dynamic_slice_in_dim(virt_energy, column * slab_width, slab_width)
    source_cube = factors.reshape(factors.shape[0], aux_local, orbital_count)

    def one_slot(position, accumulated):
        orbitals = lax.dynamic_index_in_dim(plan, position, 1, keepdims=False)
        flags = lax.dynamic_index_in_dim(enabled, position, 1, keepdims=False)
        targets_flat = orbitals.T.reshape(-1)
        picked = jnp.take(source_cube, targets_flat, axis=2)
        outgoing = picked.reshape(factors.shape[0], aux_local, 2, hosts_total)
        incoming = lax.all_to_all(outgoing, "occ", split_axis=3, concat_axis=1, tiled=True)
        both = lax.all_gather(incoming, "virt", axis=0, tiled=True)
        left = both[:, :, 0, 0]
        right = both[:, :, 1, 0]
        mine = lax.dynamic_index_in_dim(orbitals, myself, 0, keepdims=False)
        live_here = lax.dynamic_index_in_dim(flags, myself, 0, keepdims=False).astype(jnp.float32)
        left_slab = lax.dynamic_slice_in_dim(left, column * slab_width, slab_width, 0)
        right_slab = lax.dynamic_slice_in_dim(right, column * slab_width, slab_width, 0)
        couple_rows = lax.dot_general(
            left_slab, right, (((1,), (1,)), ((), ())), preferred_element_type=jnp.float32
        )
        couple_cols = lax.dot_general(
            left, right_slab, (((1,), (1,)), ((), ())), preferred_element_type=jnp.float32
        )
        energy_sum = jnp.take(occ_energy, mine[0]) + jnp.take(occ_energy, mine[1])
        ampl_rows = couple_rows / (energy_sum - slab_energy[:, None] - virt_energy[None, :])
        ampl_cols = couple_cols / (energy_sum - virt_energy[:, None] - slab_energy[None, :])
        mixed_rows = ((2.0 * ampl_rows - ampl_cols.T) * live_here).astype(jnp.bfloat16)
        mixed_cols = ((2.0 * ampl_cols - ampl_rows.T) * live_here).astype(jnp.bfloat16)
        toward_first = jnp.dot(mixed_rows, right, preferred_element_type=jnp.float32)
        toward_second = lax.dot_general(
            mixed_cols, left, (((0,), (0,)), ((), ())), preferred_element_type=jnp.float32
        )
        packed = jnp.stack(
            [toward_first.astype(jnp.bfloat16), toward_second.astype(jnp.bfloat16)], axis=2
        )
        packed = packed.reshape(slab_width, hosts_total, aux_local, 2, 1)
        returned = lax.all_to_all(packed, "occ", split_axis=1, concat_axis=4, tiled=True)
        onehot = (
            targets_flat[:, None] == jnp.arange(orbital_count, dtype=jnp.int32)[None, :]
        ).astype(jnp.bfloat16)
        added = jnp.dot(
            returned.reshape(slab_width * aux_local, 2 * hosts_total),
            onehot,
            preferred_element_type=jnp.float32,
        )
        return accumulated + added.reshape(accumulated.shape)

    start = jnp.zeros(factors.shape, jnp.float32)
    return lax.fori_loop(0, slot_count, one_slot, start)


def solution(mesh):
    in_specs = (P("virt", "occ"), P(), P(), P("occ", None), P("occ"))
    out_specs = P("virt", "occ")
    return jax.shard_map(body, mesh=mesh, in_specs=in_specs, out_specs=out_specs, check_vma=False)
```

profile of v0, /device:TPU:8, one launch (start us, length us, event | category | flops | bytes accessed | tf_op | source)
XLA Modules:
  0.0 244.5 jit_solution(16003386581368237176)
XLA Ops:
  6.5 1.1 copy.56
  8.5 0.8 reshape.178
  9.3 1.3 dynamic-slice.11
  11.4 31.4 %all-reduce = s32[640]{0:T(1024)S(1)} all-reduce(s32[640]{0:T(1024)S(1)} %add_dynamic-update-slice_fusion), channel_id=2, replica_groups=mesh['occ'=128,'virt'=4] {'occ'}, use_global_device_ids=true, to_apply=%add | all-reduce | flops 640 | bytes 5120
  44.8 0.8 gather_fusion
  45.5 2.8 %copy.69 = bf16[192,12,2,128]{3,2,0,1:T(2,128)(2,1)} copy(bf16[192,12,2,128]{0,1,3,2:T(8,128)(2,1)S(1)} %bitcast.73) | data formatting | bytes 2359296 | tf_op jit(solution)/shard_map/while/body/eval_jaxpr/jit(_take)/gather | solution.py:50
  48.3 2.3 broadcast_select_fusion
  50.6 3.2 %copy.59 = bf16[192,12,2,128]{0,2,1,3:T(2,128)(2,1)S(1)} copy(bf16[192,12,2,128]{3,2,0,1:T(2,128)(2,1)S(1)} %broadcast_select_fusion) | data formatting | bytes 2359296 | tf_op jit(solution)/shard_map/while/body/eval_jaxpr/jit(_take)/select_n | solution.py:50
  53.8 48.7 %all_to_all.41 = bf16[192,12,2,128]{0,2,1,3:T(2,128)(2,1)S(1)} all-to-all(bf16[192,12,2,128]{0,2,1,3:T(2,128)(2,1)S(1)} %copy.59), channel_id=1, replica_groups=mesh['occ'=128,'virt'=4] {'occ'}, dimensions={3} | all-to-all | bytes 2359296 | tf_op jit(solution)/shard_map/while/body/eval_jaxpr/all_to_all | solution.py:52
  102.5 4.4 %copy.60 = bf16[192,1536,2,1]{1,2,3,0:T(2,128)(2,1)} copy(bf16[192,1536,2,1]{0,2,1,3:T(2,128)(2,1)S(1)} %bitcast.74) | data formatting | bytes 2359296 | tf_op jit(solution)/shard_map/while/body/eval_jaxpr/all_to_all | solution.py:52
  107.0 0.6 fusion.44
  111.7 0.6 dynamic_slice.37
  113.0 0.6 fusion.45
  114.9 43.6 %all-gather.3.cloned.1.call-done = bf16[768,1536,2,1]{1,2,3,0:T(2,128)(2,1)} async-done(((bf16[192,1536,2,1]{1,2,3,0:T(2,128)(2,1)}), bf16[768,1536,2,1]{1,2,3,0:T(2,128)(2,1)}) %all-gather.3.cloned.1.call-update) | async-done | bytes 4718608 | tf_op jit(solution)/shard_map/while/body/eval_jaxpr/all_gather | solution.py:53
  158.5 9.6 %fusion.43 = (bf16[768,1536,1,1]{1,2,3,0:T(2,128)(2,1)S(1)}, bf16[768,1536,1,1]{1,2,3,0:T(2,128)(2,1)S(1)}) fusion(bf16[768,1536,2,1]{1,2,3,0:T(2,128)(2,1)} %all-gather.3.cloned.1.call-done), kind=kLoop, calls=%fused_computation.67 | loop fusion | bytes 9437184 | tf_op jit(solution)/shard_map/while/body/eval_jaxpr/slice | solution.py:55
  168.2 0.6 copy.70
  169.4 0.9 fusion.4
  170.3 0.9 fusion.1
  171.2 0.8 convolution_convert_fusion
  172.0 0.8 convolution_convert_fusion.1
  174.3 2.4 copy.65
  176.7 56.3 %all_to_all.42 = bf16[192,128,12,2,1]{0,3,4,2,1:T(2,128)(2,1)S(1)} all-to-all(bf16[192,128,12,2,1]{0,3,4,2,1:T(2,128)(2,1)S(1)} %copy.65), channel_id=1, replica_groups=mesh['occ'=128,'virt'=4] {'occ'}, dimensions={1} | all-to-all | bytes 2359296 | tf_op jit(solution)/shard_map/while/body/eval_jaxpr/all_to_all | solution.py:79
  233.0 2.9 %copy.66 = bf16[192,1,12,2,128,1]{4,3,2,0,5,1:T(2,128)(2,1)S(1)} copy(bf16[192,1,12,2,128,1]{0,3,2,4,5,1:T(2,128)(2,1)S(1)} %bitcast.75) | data formatting | bytes 2359296 | tf_op jit(solution)/shard_map/while/body/eval_jaxpr/all_to_all | solution.py:79
  236.5 1.1 reshape.186
  (41 shorter events, 5.1 us)
Async XLA Ops:
  6.5 152.0 %all-gather.3.cloned.1.call-start = ((), (), s32[]{:S(2)}) async-start(), calls=%async_computation.2 | async-start | bytes 5898240 | tf_op jit(solution)/shard_map/while/body/eval_jaxpr/all_gather | solution.py:53
  102.5 10.5 %copy-start.1 = (f32[64]{0:T(128)S(1)}, f32[64]{0:T(128)}, u32[]{:S(2)}) copy-start(f32[64]{0:T(128)} %param.6) | copy-start | bytes 772
  102.5 12.3 %copy-start = (f32[768]{0:T(1024)S(1)}, f32[768]{0:T(1024)}, u32[]{:S(2)}) copy-start(f32[768]{0:T(1024)} %param.7) | copy-start | bytes 9220
Sparse Core Ops, SparseCore 0:
  107.0 51.4 all-gather.2
where the time goes:
time: 245 us; the launch traced here: 244 us
  blocking collectives  136 us (56%)
  waiting for transfers between devices  43.6 us (18%)
  local copies, waits for them, and re-layouts  36 us (15%)
  between operations  20.8 us (8%)
  matrix products  3.96 us (2%)
  other arithmetic  3.7 us (2%)
    all_to_all x1, blocking collectives, one_slot(): lax.all_to_all(packed, 'occ', split_axis=1, concat_axis=4, tiled=True)  56.3 us
    all_to_all x1, blocking collectives, one_slot(): lax.all_to_all(outgoing, 'occ', split_axis=3, concat_axis=1, tiled=True)  48.7 us
    all_gather x1, waiting for transfers between devices, one_slot(): both = lax.all_gather(incoming, 'virt', axis=0, tiled=True)  43.6 us
    unnamed x1, blocking collectives  31.4 us
    slice x1, local copies, waits for them, and re-layouts, one_slot(): right = both[:, :, 1, 0]  9.63 us
  transfers between devices with their start and end apart: 1, of which 1 were waited for; matrix products, arithmetic and copies ran while one was open for 1% of the time, Pallas kernels for 0%

commit v1 on v0

--- a/solution.py
+++ b/solution.py
@@ -50,7 +50,9 @@
         picked = jnp.take(source_cube, targets_flat, axis=2)
         outgoing = picked.reshape(factors.shape[0], aux_local, 2, hosts_total)
         incoming = lax.all_to_all(outgoing, "occ", split_axis=3, concat_axis=1, tiled=True)
-        both = lax.all_gather(incoming, "virt", axis=0, tiled=True)
+        both = jnp.concatenate(
+            lax.all_to_all(jnp.stack([incoming] * lax.axis_size("virt")), "virt", 0, 0), axis=0
+        )
         left = both[:, :, 0, 0]
         right = both[:, :, 1, 0]
         mine = lax.dynamic_index_in_dim(orbitals, myself, 0, keepdims=False)

time: 245 us -> 224 us (0.914)
  between operations: 20.8 us -> 7.36 us
  local copies, waits for them, and re-layouts: 36 us -> 27.5 us
  starting transfers between devices: 0.01 us -> 5.24 us
  blocking collectives: 136 us -> 131 us
    all_to_all x0 -> x1, waiting for transfers between devices: none -> 44.7 us  [one_slot(): lax.all_to_all(jnp.stack([incoming] * lax.axis_size('virt')), 'virt', 0, 0)]
    all_gather x1 -> x0, waiting for transfers between devices: 43.6 us -> none  [one_slot(): both = lax.all_gather(incoming, 'virt', axis=0, tiled=True)]
    slice x1, local copies, waits for them, and re-layouts: 9.63 us -> 0.31 us  [one_slot(): right = both[:, :, 1, 0]]
    all_to_all x1, blocking collectives: 56.3 us -> 50.5 us  [one_slot(): lax.all_to_all(packed, 'occ', split_axis=1, concat_axis=4, tiled=True)]
    all_to_all x0 -> x1, starting transfers between devices: none -> 5.24 us  [one_slot(): lax.all_to_all(jnp.stack([incoming] * lax.axis_size('virt')), 'virt', 0, 0)]
    another operation x2 -> x4, local copies, waits for them, and re-layouts: 0.19 us -> 3.89 us  [the longest x2 3.69 us: one_slot(): jnp.stack([incoming] * lax.axis_size('virt'))]
where the time goes in v1:
time: 224 us; the launch traced here: 223 us
  blocking collectives  131 us (58%)
  waiting for transfers between devices  44.7 us (20%)
  local copies, waits for them, and re-layouts  27.5 us (12%)
  between operations  7.36 us (3%)
  starting transfers between devices  5.24 us (2%)
  matrix products  3.98 us (2%)
  other arithmetic  3.7 us (2%)
    all_to_all x1, blocking collectives, one_slot(): lax.all_to_all(packed, 'occ', split_axis=1, concat_axis=4, tiled=True)  50.5 us
    all_to_all x1, blocking collectives, one_slot(): lax.all_to_all(outgoing, 'occ', split_axis=3, concat_axis=1, tiled=True)  48.7 us
    all_to_all x1, waiting for transfers between devices, one_slot(): lax.all_to_all(jnp.stack([incoming] * lax.axis_size('virt')), 'virt', 0, 0)  44.7 us
    unnamed x1, blocking collectives  31.4 us
    all_to_all x1, starting transfers between devices, one_slot(): lax.all_to_all(jnp.stack([incoming] * lax.axis_size('virt')), 'virt', 0, 0)  5.24 us
  transfers between devices with their start and end apart: 1, of which 1 were waited for; matrix products, arithmetic and copies ran while one was open for 1% of the time, Pallas kernels for 0%

profile of v1, /device:TPU:8, one launch (start us, length us, event | category | flops | bytes accessed | tf_op | source)
XLA Modules:
  0.0 223.0 jit_solution(14506530048558283184)
XLA Ops:
  0.0 1.1 copy.48
  2.0 0.8 reshape.187
  2.8 1.3 dynamic-slice.11
  4.9 31.4 %all-reduce = s32[640]{0:T(1024)S(1)} all-reduce(s32[640]{0:T(1024)S(1)} %add_dynamic-update-slice_fusion), channel_id=2, replica_groups=mesh['occ'=128,'virt'=4] {'occ'}, use_global_device_ids=true, to_apply=%add | all-reduce | flops 640 | bytes 5120
  38.2 0.8 gather_fusion
  39.0 2.8 %copy.60 = bf16[192,12,2,128]{3,2,0,1:T(2,128)(2,1)} copy(bf16[192,12,2,128]{0,1,3,2:T(8,128)(2,1)S(1)} %bitcast.79) | data formatting | bytes 2359296 | tf_op jit(solution)/shard_map/while/body/eval_jaxpr/jit(_take)/gather | solution.py:50
  41.8 2.3 %broadcast_select_fusion = bf16[192,12,2,128]{3,2,0,1:T(2,128)(2,1)S(1)} fusion(bf16[192,12,2,128]{3,2,0,1:T(2,128)(2,1)} %copy.60, pred[2,128]{1,0:T(4,128)(4,1)S(1)} %compare_and_fusion), kind=kLoop, calls=%fused_computation.9 | loop fusion | flops 589824 | bytes 2359552 | tf_op jit(solution)/shard_map/while/body/eval_jaxpr/jit(_take)/select_n | solution.py:50
  44.1 3.2 %copy.51 = bf16[192,12,2,128]{0,2,1,3:T(2,128)(2,1)S(1)} copy(bf16[192,12,2,128]{3,2,0,1:T(2,128)(2,1)S(1)} %broadcast_select_fusion) | data formatting | bytes 2359296 | tf_op jit(solution)/shard_map/while/body/eval_jaxpr/jit(_take)/select_n | solution.py:50
  47.3 48.7 %all_to_all.44 = bf16[192,12,2,128]{0,2,1,3:T(2,128)(2,1)S(1)} all-to-all(bf16[192,12,2,128]{0,2,1,3:T(2,128)(2,1)S(1)} %copy.51), channel_id=1, replica_groups=mesh['occ'=128,'virt'=4] {'occ'}, dimensions={3} | all-to-all | bytes 2359296 | tf_op jit(solution)/shard_map/while/body/eval_jaxpr/all_to_all | solution.py:52
  96.0 1.1 copy.52
  97.1 2.6 %stack.24 = bf16[4,192,1536,2,1]{2,1,3,4,0:T(8,128)(2,1)} broadcast(bf16[192,1536,2]{1,0,2:T(8,128)(2,1)S(1)} %copy.52), dimensions={1,2,3} | broadcast | bytes 5898240 | tf_op jit(solution)/shard_map/while/body/eval_jaxpr/stack | solution.py:54
  99.7 5.2 %all-to-all-start.1 = ((bf16[4,192,1536,2,1]{2,1,3,4,0:T(8,128)(2,1)}), bf16[4,192,1536,2,1]{2,1,3,4,0:T(8,128)(2,1)}, u32[]{:S(2)}, u32[]{:S(2)}) async-start(bf16[4,192,1536,2,1]{2,1,3,4,0:T(8,128)(2,1)} %stack.24), calls=%async_computation.1 | async-start | bytes 9437184 | tf_op jit(solution)/shard_map/while/body/eval_jaxpr/all_to_all | solution.py:54
  109.5 0.6 dynamic_slice.37
  110.8 0.7 fusion.49
  112.9 44.7 %all-to-all-done.1 = bf16[4,192,1536,2,1]{2,1,3,4,0:T(8,128)(2,1)} async-done(((bf16[4,192,1536,2,1]{2,1,3,4,0:T(8,128)(2,1)}), bf16[4,192,1536,2,1]{2,1,3,4,0:T(8,128)(2,1)}, u32[]{:S(2)}, u32[]{:S(2)}) %all-to-all-start.1) | async-done | bytes 4718624 | tf_op jit(solution)/shard_map/while/body/eval_jaxpr/all_to_all | solution.py:54
  157.6 2.6 %copy.53 = bf16[4,192,1536,2,1]{2,1,0,3,4:T(8,128)(2,1)S(1)} copy(bf16[4,192,1536,2,1]{2,1,3,4,0:T(8,128)(2,1)} %all-to-all-done.1) | data formatting | bytes 9437184 | tf_op jit(solution)/shard_map/while/body/eval_jaxpr/all_to_all | solution.py:54
  160.5 0.9 fusion.4
  161.5 0.9 fusion.1
  162.4 0.8 convolution_convert_fusion
  163.2 0.8 convolution_convert_fusion.1
  165.5 2.4 %copy.56 = bf16[192,128,12,2,1]{0,3,4,2,1:T(2,128)(2,1)S(1)} copy(bf16[192,128,12,2,1]{0,2,1,4,3:T(8,128)(2,1)S(1)} %pad_maximum_fusion) | data formatting | bytes 2359296 | tf_op jit(solution)/shard_map/while/body/eval_jaxpr/stack | solution.py:77
  167.9 50.5 %all_to_all.45 = bf16[192,128,12,2,1]{0,3,4,2,1:T(2,128)(2,1)S(1)} all-to-all(bf16[192,128,12,2,1]{0,3,4,2,1:T(2,128)(2,1)S(1)} %copy.56), channel_id=1, replica_groups=mesh['occ'=128,'virt'=4] {'occ'}, dimensions={1} | all-to-all | bytes 2359296 | tf_op jit(solution)/shard_map/while/body/eval_jaxpr/all_to_all | solution.py:81
  218.4 2.9 %copy.57 = bf16[192,1,12,2,128,1]{4,3,2,0,5,1:T(2,128)(2,1)S(1)} copy(bf16[192,1,12,2,128,1]{0,3,2,4,5,1:T(2,128)(2,1)S(1)} %bitcast.81) | data formatting | bytes 2359296 | tf_op jit(solution)/shard_map/while/body/eval_jaxpr/all_to_all | solution.py:81
  221.9 1.1 reshape.196
  (40 shorter events, 5.4 us)
Async XLA Ops:
  99.7 11.1 %copy-start.1 = (f32[64]{0:T(128)S(1)}, f32[64]{0:T(128)}, u32[]{:S(2)}) copy-start(f32[64]{0:T(128)} %param.6) | copy-start | bytes 772
  99.7 13.1 %copy-start = (f32[768]{0:T(1024)S(1)}, f32[768]{0:T(1024)}, u32[]{:S(2)}) copy-start(f32[768]{0:T(1024)} %param.7) | copy-start | bytes 9220
  99.7 57.9 %all-to-all-start.1 = ((bf16[4,192,1536,2,1]{2,1,3,4,0:T(8,128)(2,1)}), bf16[4,192,1536,2,1]{2,1,3,4,0:T(8,128)(2,1)}, u32[]{:S(2)}, u32[]{:S(2)}) async-start(bf16[4,192,1536,2,1]{2,1,3,4,0:T(8,128)(2,1)} %stack.24), calls=%async_computation.1 | async-start | bytes 9437184 | tf_op jit(solution)/shard_map/while/body/eval_jaxpr/all_to_all | solution.py:54
